TPU v7x, 32 devices: a whole 2x2x4 slice. The times are simulated.
32 devices in a mesh: space: 4 (over y, x), vel: 8 (over z, core).
Axes of the slice: x: 2, y: 2, z: 4, core: 2. Of those that a mesh axis runs over, the one named last changes fastest.
Arguments:
- cotangent: float32 [8192, 128, 128], P('vel', 'space'), may hold values from -6 to 6
- speed: float32 [3, 8192], P(None, 'vel'), may hold values from 0.1 to 3
- direction: int32 [3, 8192], P(None, 'vel'), may hold values from 0 to 1
- macroscopic_record: float32 [3, 5, 128, 128], P(None, None, 'space'), may hold values from -1 to 2, as said below
Outputs:
- gradient: float32 [8192, 128, 128], P('vel', 'space')
Inputs may be any that keep to these rules, and one draw needn't show every extreme that they name: `direction`: 1 marks a positive velocity component, 0 a negative one. `macroscopic_record`: density and temperature lie between 0.5 and 2, flow velocity components between -1 and 1.
All inputs are finite; a program needn't handle non-finite values.
Results may differ from a plain program's by a relative error of at most 0.00013.
Values sent between devices are 32-bit elements; how exact they have to be, the bound alone decides.
No kernel may reach another device: no remote copies, remote signals or barrier semaphores. Data moves between devices by JAX's collectives and lax.ppermute only.
A program may use at most 128 MiB of HBM per device.

v0:
```python
import math
import jax
import jax.numpy as jnp
from jax import lax
from jax.sharding import PartitionSpec as P

SPEED_POINTS = 8192
STEPS = 3
courant_number = 0.1
region_capacity = 216.0
mode_gains = (
    1.0,
    1.0,
    1.0,
    1.0,
    1.0,
    -0.5,
    -0.5,
    -0.5,
    -0.5,
    -0.5,
    1.0 / 3.0,
    1.0 / 3.0,
    1.0 / 3.0,
)
monomials = [
    (first, second, degree - first - second)
    for degree in range(4)
    for first in range(degree, -1, -1)
    for second in range(degree - first, -1, -1)
]
monomial_place = {exponents: place for place, exponents in enumerate(monomials)}


def with_halo(x, sides, width):
    for axis, dim in sides:
        peers, length = (lax.axis_size(axis), x.shape[dim])
        up = [(i, (i + 1) % peers) for i in range(peers)]
        down = [(j, i) for i, j in up]
        last = lax.slice_in_dim(x, length - width, length, axis=dim)
        first = lax.slice_in_dim(x, 0, width, axis=dim)
        before = lax.ppermute(last, axis, up)
        after = lax.ppermute(first, axis, down)
        x = jnp.concatenate([before, x, after], axis=dim)
    return x


def raise_to(values, exponent):
    result = jnp.ones_like(values)
    for repeat in range(exponent):
        result = result * values
    return result


def poly_mul(left, right):
    result = {}
    for left_key, left_coef in left.items():
        for right_key, right_coef in right.items():
            joined = (
                left_key[0] + right_key[0],
                left_key[1] + right_key[1],
                left_key[2] + right_key[2],
            )
            product = left_coef * right_coef
            result[joined] = result[joined] + product if joined in result else product
    return result


def poly_comb(terms):
    result = {}
    for weight, poly in terms:
        for poly_key, poly_coef in poly.items():
            scaled = weight * poly_coef
            result[poly_key] = result[poly_key] + scaled if poly_key in result else scaled
    return result


def hermite_polys(flow_rows, reciprocal_factor):
    linear = []
    for component in range(3):
        unit_key = tuple((1 if other == component else 0 for other in range(3)))
        linear.append(
            {unit_key: reciprocal_factor, (0, 0, 0): -flow_rows[component] * reciprocal_factor}
        )
    comp_x, comp_y, comp_z = linear
    unit_poly = {(0, 0, 0): 1.0}
    square_x = poly_mul(comp_x, comp_x)
    square_y = poly_mul(comp_y, comp_y)
    square_z = poly_mul(comp_z, comp_z)
    square = poly_comb([(1.0, square_x), (1.0, square_y), (1.0, square_z)])
    shifted = poly_comb([(1.0, square), (-5.0, unit_poly)])
    heat_scale = 1.0 / math.sqrt(10.0)
    return [
        unit_poly,
        comp_x,
        comp_y,
        comp_z,
        poly_comb([(1.0 / math.sqrt(6.0), square), (-3.0 / math.sqrt(6.0), unit_poly)]),
        poly_mul(comp_x, comp_y),
        poly_mul(comp_x, comp_z),
        poly_mul(comp_y, comp_z),
        poly_comb([(0.5, square_x), (-0.5, square_y)]),
        poly_comb(
            [
                (1.0 / math.sqrt(12.0), square_x),
                (1.0 / math.sqrt(12.0), square_y),
                (-2.0 / math.sqrt(12.0), square_z),
            ]
        ),
        poly_comb([(heat_scale, poly_mul(comp_x, shifted))]),
        poly_comb([(heat_scale, poly_mul(comp_y, shifted))]),
        poly_comb([(heat_scale, poly_mul(comp_z, shifted))]),
    ]


def to_modes(raw_rows, polys, zeros_like):
    mode_rows = []
    for poly in polys:
        running = zeros_like
        for poly_key, poly_coef in poly.items():
            running = running + poly_coef * raw_rows[monomial_place[poly_key]]
        mode_rows.append(running)
    return mode_rows


def to_coeffs(mode_rows, polys, zeros_like):
    coeff_rows = [zeros_like for exponents in monomials]
    for mode_index, poly in enumerate(polys):
        scaled_mode = mode_gains[mode_index] * mode_rows[mode_index]
        for poly_key, poly_coef in poly.items():
            place = monomial_place[poly_key]
            coeff_rows[place] = coeff_rows[place] + poly_coef * scaled_mode
    return jnp.stack(coeff_rows)


def pad_both(values, along):
    extent = values.shape[along]
    lower_rim = lax.slice_in_dim(values, extent - 2, extent, axis=along)
    upper_rim = lax.slice_in_dim(values, 0, 2, axis=along)
    return jnp.concatenate([lower_rim, values, upper_rim], axis=along)


def upwind_back(padded, length, along, lam_col, positive):

    def window(start_at):
        return lax.slice_in_dim(padded, start_at, start_at + length, axis=along)

    center = window(2)
    nearer = jnp.where(positive, window(3), window(1))
    farther = jnp.where(positive, window(4), window(0))
    return center - 0.5 * lam_col * (3.0 * center - 4.0 * nearer + farther)


def shards(cotangent, speed, direction, macroscopic_record):
    rows_x = cotangent.shape[1]
    cols_y = cotangent.shape[2]
    velocity = (2 * direction - 1).astype(jnp.float32) * speed
    factors = courant_number * speed
    positive = direction > 0
    lam_x = factors[0][:, None, None]
    lam_y = factors[1][:, None, None]
    pos_x = positive[0][:, None, None]
    pos_y = positive[1][:, None, None]
    table = jnp.stack(
        [
            raise_to(velocity[0], exponents[0])
            * raise_to(velocity[1], exponents[1])
            * raise_to(velocity[2], exponents[2])
            for exponents in monomials
        ]
    )
    adjoint = cotangent
    for iteration_counter in range(STEPS - 1, -1, -1):
        moved_y = upwind_back(pad_both(adjoint, 2), cols_y, 2, lam_y, pos_y)
        padded_x = with_halo(moved_y, (("space", 1),), 2)
        advected = upwind_back(padded_x, rows_x, 1, lam_x, pos_x)
        particle_concentration = macroscopic_record[iteration_counter, 0]
        flow_rows = [macroscopic_record[iteration_counter, 1 + component] for component in range(3)]
        thermal_energy_level = macroscopic_record[iteration_counter, 4]
        reciprocal_factor = 1.0 / jnp.sqrt(thermal_energy_level)
        normalising_coefficient = (
            particle_concentration
            * (2.0 * math.pi * thermal_energy_level) ** (-1.5)
            * region_capacity
            / SPEED_POINTS
        )
        relaxation_rate = 0.3 * particle_concentration * jnp.sqrt(thermal_energy_level)
        peculiar = [
            (velocity[component][:, None, None] - flow_rows[component]) * reciprocal_factor
            for component in range(3)
        ]
        weight = normalising_coefficient * jnp.exp(
            -0.5 * (peculiar[0] ** 2 + peculiar[1] ** 2 + peculiar[2] ** 2)
        )
        raw_moments = jnp.einsum(
            "av,vxy->axy", table, weight * advected, precision=lax.Precision.HIGHEST
        )
        zero_cells = jnp.zeros_like(particle_concentration)
        summed = lax.psum(raw_moments, "vel")
        polys = hermite_polys(flow_rows, reciprocal_factor)
        coeffs = to_coeffs(to_modes(summed, polys, zero_cells), polys, zero_cells)
        returned = jnp.einsum("av,axy->vxy", table, coeffs, precision=lax.Precision.HIGHEST)
        adjoint = (1.0 - relaxation_rate) * advected + relaxation_rate * returned
    return adjoint


def solution(mesh):
    in_specs = (
        P("vel", "space", None),
        P(None, "vel"),
        P(None, "vel"),
        P(None, None, "space", None),
    )
    out_specs = P("vel", "space", None)
    return jax.shard_map(shards, mesh=mesh, in_specs=in_specs, out_specs=out_specs, check_vma=False)
```

profile of v0, /device:TPU:0, one launch (start us, length us, event | category | flops | bytes accessed | tf_op | source)
XLA Modules:
  0.0 712.7 jit_solution(4509849928719995497)
XLA Ops:
  6.5 0.7 broadcast_compare_fusion
  7.3 0.7 convert_multiply_fusion
  8.0 16.5 %copy.21 = f32[1024,32,128]{0,2,1:T(8,128)} copy(f32[1024,32,128]{2,1,0:T(8,128)} %param.4) | data formatting | bytes 33554432 | tf_op args[0]
  24.6 1.8 fusion.371
  26.3 0.6 slice_multiply_fusion.27
  26.9 34.9 %fusion.46 = f32[1024,32,128]{0,2,1:T(8,128)} fusion(f32[1024,32,128]{0,2,1:T(8,128)} %copy.21, f32[1024,32,2]{0,2,1:T(2,128)S(1)} %get-tuple-element.47, f32[1024,32,2]{0,2,1:T(2,128)S(1)} %get-tuple-element.46, f32[1024]{0:T(1024)S(1)} %bitcast.1794, pred[1024]{0:T(1024)(128)(4,1)S(1)} %get-tuple-element.6), kind=kLoop, calls=%fused_computation.70 | loop fusion | flops 50331648 | bytes 34083840 | tf_op jit(solution)/shard_map/sub | solution.py:151
  61.8 2.8 fusion.370
  64.6 3.9 collective-permute-start
  68.5 0.6 slice_multiply_fusion.34
  69.1 1.5 stack.12
  70.7 0.7 multiply_bitcast_fusion
  71.3 21.0 %collective-permute-done = f32[1024,2,128]{0,2,1:T(8,128)S(1)} collective-permute-done((f32[1024,2,128]{0,2,1:T(8,128)}, f32[1024,2,128]{0,2,1:T(8,128)S(1)}, u32[]{:S(2)}, u32[]{:S(2)}) %collective-permute-start) | collective-permute-done | bytes 1048608 | tf_op jit(solution)/shard_map/ppermute | solution.py:43
  92.3 22.2 %collective-permute-done.1 = f32[1024,2,128]{0,2,1:T(8,128)S(1)} collective-permute-done((f32[1024,2,128]{0,2,1:T(8,128)S(1)}, f32[1024,2,128]{0,2,1:T(8,128)S(1)}, u32[]{:S(2)}, u32[]{:S(2)}) %collective-permute-start.1) | collective-permute-done | bytes 1048608 | tf_op jit(solution)/shard_map/ppermute | solution.py:42
  114.6 27.7 %fusion.38 = f32[1024,32,128]{0,2,1:T(8,128)S(1)} fusion(f32[1024,32,128]{0,2,1:T(8,128)} %fusion.46, f32[1024,2,128]{0,2,1:T(8,128)S(1)} %collective-permute-done.1, f32[1024,2,128]{0,2,1:T(8,128)S(1)} %collective-permute-done, f32[1024]{0:T(1024)S(1)} %bitcast.1791, pred[1024]{0:T(1024)(128)(4,1)S(1)} %get-tuple-element.5), kind=kLoop, calls=%fused_computation.62 | loop fusion | flops 50331648 | bytes 35656704 | tf_op jit(solution)/shard_map/sub | solution.py:151
  142.3 23.4 %fusion.86 = f32[20,32,128]{2,0,1:T(8,128)S(1)} fusion(f32[1024,32,128]{0,2,1:T(8,128)S(1)} %fusion.38, f32[32,128]{1,0:T(8,128)S(1)} %get-tuple-element.55, f32[1024]{0:T(1024)S(1)} %bitcast.1803, f32[32,128]{1,0:T(8,128)S(1)} %get-tuple-element.56, f32[1024]{0:T(1024)S(1)} %bitcast.1800, f32[32,128]{1,0:T(8,128)S(1)} %get-tuple-element.58, ...), kind=kOutput, calls=%fused_computation.125 | convolution fusion | flops 1065353216 | bytes 17281024 | tf_op jit(solution)/shard_map/av,vxy->axy/dot_general | solution.py:195
  165.7 0.8 copy.23
  166.5 0.5 all-reduce.6.cloned.1.call-start
  167.0 55.6 %all-reduce.4.cloned.1.call-done = f32[20,32,128]{2,1,0:T(8,128)} async-done(((f32[20,32,128]{2,1,0:T(8,128)}), f32[20,32,128]{2,1,0:T(8,128)}) %all-reduce.4.cloned.1.call-update) | async-done | bytes 327696 | tf_op jit(solution)/shard_map/psum | solution.py:199
  222.6 1.1 constant_dynamic-update-slice_fusion.19
  223.7 0.9 constant_dynamic-update-slice_fusion.18
  224.6 0.9 constant_dynamic-update-slice_fusion.17
  225.4 0.9 constant_dynamic-update-slice_fusion.16
  226.3 0.8 constant_dynamic-update-slice_fusion.14
  227.1 0.8 constant_dynamic-update-slice_fusion.13
  227.9 0.8 constant_dynamic-update-slice_fusion.11
  229.0 17.5 %multiply_add_fusion.2 = f32[1024,32,128]{0,2,1:T(8,128)S(1)} fusion(f32[1024,32,128]{0,2,1:T(8,128)} %copy-done.2, f32[32,128]{1,0:T(8,128)S(1)} %get-tuple-element.64, f32[32,128]{1,0:T(8,128)S(1)} %get-tuple-element.63, f32[20,32,128]{2,1,0:T(8,128)S(1)} %constant_dynamic-update-slice_fusion, f32[20,1024]{1,0:T(8,128)S(1)} %stack.12), kind=kOutput, calls=%fused_computation.124 | convolution fusion | flops 1019215872 | bytes 33996800 | tf_op jit(solution)/shard_map/av,axy->vxy/dot_general | solution.py:202
  246.5 6.2 copy-done.1
  252.9 34.8 %fusion.30 = f32[1024,32,128]{0,2,1:T(8,128)} fusion(f32[1024,32,128]{0,2,1:T(8,128)} %copy-done.1, f32[1024,32,2]{0,2,1:T(2,128)S(1)} %get-tuple-element.43, f32[1024,32,2]{0,2,1:T(2,128)S(1)} %get-tuple-element.42, f32[1024]{0:T(1024)S(1)} %bitcast.1795, pred[1024]{0:T(1024)(128)(4,1)S(1)} %get-tuple-element.6), kind=kLoop, calls=%fused_computation.54 | loop fusion | flops 50331648 | bytes 34083840 | tf_op jit(solution)/shard_map/sub | solution.py:151
  287.7 1.7 fusion.368
  289.4 2.4 collective-permute-start.2
  292.0 23.4 %collective-permute-done.2 = f32[1024,2,128]{0,2,1:T(8,128)S(1)} collective-permute-done((f32[1024,2,128]{0,2,1:T(8,128)S(1)}, f32[1024,2,128]{0,2,1:T(8,128)S(1)}, u32[]{:S(2)}, u32[]{:S(2)}) %collective-permute-start.2) | collective-permute-done | bytes 1048608 | tf_op jit(solution)/shard_map/ppermute | solution.py:43
  315.4 20.5 %collective-permute-done.3 = f32[1024,2,128]{0,2,1:T(8,128)S(1)} collective-permute-done((f32[1024,2,128]{0,2,1:T(8,128)S(1)}, f32[1024,2,128]{0,2,1:T(8,128)S(1)}, u32[]{:S(2)}, u32[]{:S(2)}) %collective-permute-start.3) | collective-permute-done | bytes 1048608 | tf_op jit(solution)/shard_map/ppermute | solution.py:42
  335.9 27.7 %fusion.22 = f32[1024,32,128]{0,2,1:T(8,128)S(1)} fusion(f32[1024,32,128]{0,2,1:T(8,128)} %fusion.30, f32[1024,2,128]{0,2,1:T(8,128)S(1)} %collective-permute-done.3, f32[1024,2,128]{0,2,1:T(8,128)S(1)} %collective-permute-done.2, f32[1024]{0:T(1024)S(1)} %bitcast.1792, pred[1024]{0:T(1024)(128)(4,1)S(1)} %get-tuple-element.5), kind=kLoop, calls=%fused_computation.46 | loop fusion | flops 50331648 | bytes 35656704 | tf_op jit(solution)/shard_map/sub | solution.py:151
  363.7 23.4 %fusion.70 = f32[20,32,128]{2,0,1:T(8,128)S(1)} fusion(f32[1024,32,128]{0,2,1:T(8,128)S(1)} %fusion.22, f32[32,128]{1,0:T(8,128)S(1)} %copy-done.9, f32[32,128]{1,0:T(8,128)S(1)} %copy-done.10, f32[32,128]{1,0:T(8,128)S(1)} %copy-done.12, f32[32,128]{1,0:T(8,128)S(1)} %copy-done.11, f32[32,128]{1,0:T(8,128)S(1)} %copy-done.8, f32[1024]{0:T(1024)S(1)} %bitcast.1804, ...), kind=kOutput, calls=%fused_computation.108 | convolution fusion | flops 1065353216 | bytes 17281024 | tf_op jit(solution)/shard_map/av,vxy->axy/dot_general | solution.py:195
  387.1 0.8 copy.26
  387.9 0.3 all-reduce.8.cloned.1.call-start
  388.1 54.6 %all-reduce.6.cloned.1.call-done = f32[20,32,128]{2,1,0:T(8,128)} async-done(((f32[20,32,128]{2,1,0:T(8,128)}), f32[20,32,128]{2,1,0:T(8,128)}) %all-reduce.6.cloned.1.call-update) | async-done | bytes 327696 | tf_op jit(solution)/shard_map/psum | solution.py:199
  442.7 1.1 constant_dynamic-update-slice_fusion.39
  443.8 0.9 constant_dynamic-update-slice_fusion.38
  444.7 0.9 constant_dynamic-update-slice_fusion.37
  445.5 0.9 constant_dynamic-update-slice_fusion.36
  446.4 0.8 constant_dynamic-update-slice_fusion.34
  447.2 0.8 constant_dynamic-update-slice_fusion.33
  448.1 0.8 constant_dynamic-update-slice_fusion.31
  449.1 17.5 %multiply_add_fusion.1 = f32[1024,32,128]{0,2,1:T(8,128)S(1)} fusion(f32[1024,32,128]{0,2,1:T(8,128)} %copy-done.4, f32[32,128]{1,0:T(8,128)S(1)} %get-tuple-element.66, f32[32,128]{1,0:T(8,128)S(1)} %get-tuple-element.65, f32[20,32,128]{2,1,0:T(8,128)S(1)} %constant_dynamic-update-slice_fusion.20, f32[20,1024]{1,0:T(8,128)S(1)} %stack.12), kind=kOutput, calls=%fused_computation.107 | convolution fusion | flops 1019215872 | bytes 33996800 | tf_op jit(solution)/shard_map/av,axy->vxy/dot_general | solution.py:202
  466.6 6.2 copy-done
  473.0 34.8 %fusion.14 = f32[1024,32,128]{0,2,1:T(8,128)} fusion(f32[1024,32,128]{0,2,1:T(8,128)} %copy-done, f32[1024,32,2]{0,2,1:T(2,128)S(1)} %get-tuple-element.39, f32[1024,32,2]{0,2,1:T(2,128)S(1)} %get-tuple-element.38, f32[1024]{0:T(1024)S(1)} %bitcast.1796, pred[1024]{0:T(1024)(128)(4,1)S(1)} %get-tuple-element.6), kind=kLoop, calls=%fused_computation.38 | loop fusion | flops 50331648 | bytes 34083840 | tf_op jit(solution)/shard_map/sub | solution.py:151
  507.8 1.7 fusion.366
  509.5 2.4 collective-permute-start.4
  512.2 23.4 %collective-permute-done.4 = f32[1024,2,128]{0,2,1:T(8,128)S(1)} collective-permute-done((f32[1024,2,128]{0,2,1:T(8,128)S(1)}, f32[1024,2,128]{0,2,1:T(8,128)S(1)}, u32[]{:S(2)}, u32[]{:S(2)}) %collective-permute-start.4) | collective-permute-done | bytes 1048608 | tf_op jit(solution)/shard_map/ppermute | solution.py:43
  535.6 20.5 %collective-permute-done.5 = f32[1024,2,128]{0,2,1:T(8,128)S(1)} collective-permute-done((f32[1024,2,128]{0,2,1:T(8,128)S(1)}, f32[1024,2,128]{0,2,1:T(8,128)S(1)}, u32[]{:S(2)}, u32[]{:S(2)}) %collective-permute-start.5) | collective-permute-done | bytes 1048608 | tf_op jit(solution)/shard_map/ppermute | solution.py:42
  556.1 27.7 %fusion.6 = f32[1024,32,128]{0,2,1:T(8,128)S(1)} fusion(f32[1024,32,128]{0,2,1:T(8,128)} %fusion.14, f32[1024,2,128]{0,2,1:T(8,128)S(1)} %collective-permute-done.5, f32[1024,2,128]{0,2,1:T(8,128)S(1)} %collective-permute-done.4, f32[1024]{0:T(1024)S(1)} %bitcast.1793, pred[1024]{0:T(1024)(128)(4,1)S(1)} %get-tuple-element.5), kind=kLoop, calls=%fused_computation.30 | loop fusion | flops 50331648 | bytes 35656704 | tf_op jit(solution)/shard_map/sub | solution.py:151
  583.8 23.4 %fusion.54 = f32[20,32,128]{2,0,1:T(8,128)S(1)} fusion(f32[1024,32,128]{0,2,1:T(8,128)S(1)} %fusion.6, f32[32,128]{1,0:T(8,128)S(1)} %copy-done.6, f32[32,128]{1,0:T(8,128)S(1)} %copy-done.7, f32[32,128]{1,0:T(8,128)S(1)} %get-tuple-element.60, f32[32,128]{1,0:T(8,128)S(1)} %get-tuple-element.51, f32[32,128]{1,0:T(8,128)S(1)} %get-tuple-element.48, ...), kind=kOutput, calls=%fused_computation.91 | convolution fusion | flops 1065353216 | bytes 17281024 | tf_op jit(solution)/shard_map/av,vxy->axy/dot_general | solution.py:195
  607.2 0.8 copy.29
  608.0 54.9 %all-reduce.8.cloned.1.call-done = f32[20,32,128]{2,1,0:T(8,128)} async-done(((f32[20,32,128]{2,1,0:T(8,128)}), f32[20,32,128]{2,1,0:T(8,128)}) %all-reduce.8.cloned.1.call-update) | async-done | bytes 327696 | tf_op jit(solution)/shard_map/psum | solution.py:199
  662.8 1.1 constant_dynamic-update-slice_fusion.59
  663.9 0.9 constant_dynamic-update-slice_fusion.58
  664.8 0.9 constant_dynamic-update-slice_fusion.57
  665.6 0.9 constant_dynamic-update-slice_fusion.56
  666.5 0.8 constant_dynamic-update-slice_fusion.54
  667.3 0.8 constant_dynamic-update-slice_fusion.53
  668.2 0.8 constant_dynamic-update-slice_fusion.51
  669.2 19.1 %multiply_add_fusion = f32[1024,32,128]{0,2,1:T(8,128)} fusion(f32[1024,32,128]{0,2,1:T(8,128)} %copy-done.3, f32[32,128]{1,0:T(8,128)S(1)} %get-tuple-element.15, f32[32,128]{1,0:T(8,128)S(1)} %get-tuple-element.14, f32[20,32,128]{2,1,0:T(8,128)S(1)} %constant_dynamic-update-slice_fusion.40, f32[20,1024]{1,0:T(8,128)S(1)} %stack.12), kind=kOutput, calls=%fused_computation.90 | convolution fusion | flops 1019215872 | bytes 33996800 | tf_op jit(solution)/shard_map/av,axy->vxy/dot_general | solution.py:202
  688.3 17.4 %copy.32 = f32[1024,32,128]{2,1,0:T(8,128)} copy(f32[1024,32,128]{0,2,1:T(8,128)} %multiply_add_fusion) | data formatting | bytes 33554432 | tf_op jit(solution)/shard_map/add | solution.py:203
  (81 shorter events, 1.7 us)
Async XLA Ops:
  6.5 216.1 %all-reduce.4.cloned.1.call-start = ((), (), s32[]{:S(2)}) async-start(), calls=%async_computation | async-start | bytes 655360 | tf_op jit(solution)/shard_map/psum | solution.py:199
  26.9 43.7 %copy-start.5 = (f32[3,5,32,128]{3,2,1,0:T(8,128)S(1)}, f32[3,5,32,128]{3,2,1,0:T(8,128)}, u32[]{:S(2)}) copy-start(f32[3,5,32,128]{3,2,1,0:T(8,128)} %param.7) | copy-start | bytes 737284
  64.6 27.8 %collective-permute-start = (f32[1024,2,128]{0,2,1:T(8,128)}, f32[1024,2,128]{0,2,1:T(8,128)S(1)}, u32[]{:S(2)}, u32[]{:S(2)}) collective-permute-start(f32[1024,2,128]{0,2,1:T(8,128)} %get-tuple-element.44), channel_id=1, source_target_pairs={{8,0},{16,8},{24,16},{0,24},{9,1},{17,9},{25,17},{1,25},{10,2},{18... | collective-permute-start | bytes 3145736 | tf_op jit(solution)/shard_map/ppermute | solution.py:43
  68.5 46.1 %collective-permute-start.1 = (f32[1024,2,128]{0,2,1:T(8,128)S(1)}, f32[1024,2,128]{0,2,1:T(8,128)S(1)}, u32[]{:S(2)}, u32[]{:S(2)}) collective-permute-start(f32[1024,2,128]{0,2,1:T(8,128)S(1)} %get-tuple-element.45), channel_id=1, source_target_pairs={{0,8},{8,16},{16,24},{24,0},{1,9},{9,17},{17,25},{25,1},{2,10},{10... | collective-permute-start | bytes 3145736 | tf_op jit(solution)/shard_map/ppermute | solution.py:42
  114.6 27.7 %copy-start.13 = (f32[1,1024]{1,0:T(1,128)S(1)}, f32[1,1024]{1,0:T(1,128)}, u32[]{:S(2)}) copy-start(f32[1,1024]{1,0:T(1,128)} %get-tuple-element.88) | copy-start | bytes 12292
  114.6 27.7 %copy-start.14 = (f32[1,1024]{1,0:T(1,128)S(1)}, f32[1,1024]{1,0:T(1,128)}, u32[]{:S(2)}) copy-start(f32[1,1024]{1,0:T(1,128)} %get-tuple-element.89) | copy-start | bytes 12292
  114.6 27.7 %copy-start.15 = (f32[1,1024]{1,0:T(1,128)S(1)}, f32[1,1024]{1,0:T(1,128)}, u32[]{:S(2)}) copy-start(f32[1,1024]{1,0:T(1,128)} %get-tuple-element.90) | copy-start | bytes 12292
  142.2 23.4 %copy-start.2 = (f32[1024,32,128]{0,2,1:T(8,128)}, f32[1024,32,128]{0,2,1:T(8,128)S(1)}, u32[]{:S(2)}) copy-start(f32[1024,32,128]{0,2,1:T(8,128)S(1)} %fusion.38) | copy-start | bytes 50331652
  166.5 276.3 %all-reduce.6.cloned.1.call-start = ((), (), s32[]{:S(2)}) async-start(), calls=%async_computation.1 | async-start | bytes 655360 | tf_op jit(solution)/shard_map/psum | solution.py:199
  246.5 6.2 copy-start.1
  289.4 26.1 %collective-permute-start.2 = (f32[1024,2,128]{0,2,1:T(8,128)S(1)}, f32[1024,2,128]{0,2,1:T(8,128)S(1)}, u32[]{:S(2)}, u32[]{:S(2)}) collective-permute-start(f32[1024,2,128]{0,2,1:T(8,128)S(1)} %get-tuple-element.40), channel_id=1, source_target_pairs={{8,0},{16,8},{24,16},{0,24},{9,1},{17,9},{25,17},{1,25},{10,2},{18... | collective-permute-start | bytes 3145736 | tf_op jit(solution)/shard_map/ppermute | solution.py:43
  291.8 71.8 %copy-start.8 = (f32[32,128]{1,0:T(8,128)S(1)}, f32[32,128]{1,0:T(8,128)}, u32[]{:S(2)}) copy-start(f32[32,128]{1,0:T(8,128)} %get-tuple-element.49) | copy-start | bytes 49156
  291.8 71.9 %copy-start.9 = (f32[32,128]{1,0:T(8,128)S(1)}, f32[32,128]{1,0:T(8,128)}, u32[]{:S(2)}) copy-start(f32[32,128]{1,0:T(8,128)} %get-tuple-element.52) | copy-start | bytes 49156
  291.8 71.9 %copy-start.10 = (f32[32,128]{1,0:T(8,128)S(1)}, f32[32,128]{1,0:T(8,128)}, u32[]{:S(2)}) copy-start(f32[32,128]{1,0:T(8,128)} %get-tuple-element.53) | copy-start | bytes 49156
  291.8 71.9 %copy-start.11 = (f32[32,128]{1,0:T(8,128)S(1)}, f32[32,128]{1,0:T(8,128)}, u32[]{:S(2)}) copy-start(f32[32,128]{1,0:T(8,128)} %get-tuple-element.54) | copy-start | bytes 49156
  291.8 71.9 %copy-start.12 = (f32[32,128]{1,0:T(8,128)S(1)}, f32[32,128]{1,0:T(8,128)}, u32[]{:S(2)}) copy-start(f32[32,128]{1,0:T(8,128)} %get-tuple-element.59) | copy-start | bytes 49156
  291.8 44.1 %collective-permute-start.3 = (f32[1024,2,128]{0,2,1:T(8,128)S(1)}, f32[1024,2,128]{0,2,1:T(8,128)S(1)}, u32[]{:S(2)}, u32[]{:S(2)}) collective-permute-start(f32[1024,2,128]{0,2,1:T(8,128)S(1)} %get-tuple-element.41), channel_id=1, source_target_pairs={{0,8},{8,16},{16,24},{24,0},{1,9},{9,17},{17,25},{25,1},{2,10},{10... | collective-permute-start | bytes 3145736 | tf_op jit(solution)/shard_map/ppermute | solution.py:42
  363.6 23.5 %copy-start.4 = (f32[1024,32,128]{0,2,1:T(8,128)}, f32[1024,32,128]{0,2,1:T(8,128)S(1)}, u32[]{:S(2)}) copy-start(f32[1024,32,128]{0,2,1:T(8,128)S(1)} %fusion.22) | copy-start | bytes 50331652
  387.9 275.0 %all-reduce.8.cloned.1.call-start = ((), (), s32[]{:S(2)}) async-start(), calls=%async_computation.2 | async-start | bytes 655360 | tf_op jit(solution)/shard_map/psum | solution.py:199
  466.6 6.2 copy-start
  509.5 26.1 %collective-permute-start.4 = (f32[1024,2,128]{0,2,1:T(8,128)S(1)}, f32[1024,2,128]{0,2,1:T(8,128)S(1)}, u32[]{:S(2)}, u32[]{:S(2)}) collective-permute-start(f32[1024,2,128]{0,2,1:T(8,128)S(1)} %get-tuple-element.36), channel_id=1, source_target_pairs={{8,0},{16,8},{24,16},{0,24},{9,1},{17,9},{25,17},{1,25},{10,2},{18... | collective-permute-start | bytes 3145736 | tf_op jit(solution)/shard_map/ppermute | solution.py:43
  511.9 71.8 %copy-start.6 = (f32[32,128]{1,0:T(8,128)S(1)}, f32[32,128]{1,0:T(8,128)}, u32[]{:S(2)}) copy-start(f32[32,128]{1,0:T(8,128)} %get-tuple-element.61) | copy-start | bytes 49156
  511.9 71.9 %copy-start.7 = (f32[32,128]{1,0:T(8,128)S(1)}, f32[32,128]{1,0:T(8,128)}, u32[]{:S(2)}) copy-start(f32[32,128]{1,0:T(8,128)} %get-tuple-element.62) | copy-start | bytes 49156
  511.9 44.2 %collective-permute-start.5 = (f32[1024,2,128]{0,2,1:T(8,128)S(1)}, f32[1024,2,128]{0,2,1:T(8,128)S(1)}, u32[]{:S(2)}, u32[]{:S(2)}) collective-permute-start(f32[1024,2,128]{0,2,1:T(8,128)S(1)} %get-tuple-element.37), channel_id=1, source_target_pairs={{0,8},{8,16},{16,24},{24,0},{1,9},{9,17},{17,25},{25,1},{2,10},{10... | collective-permute-start | bytes 3145736 | tf_op jit(solution)/shard_map/ppermute | solution.py:42
  583.7 23.4 %copy-start.3 = (f32[1024,32,128]{0,2,1:T(8,128)}, f32[1024,32,128]{0,2,1:T(8,128)S(1)}, u32[]{:S(2)}) copy-start(f32[1024,32,128]{0,2,1:T(8,128)S(1)} %fusion.6) | copy-start | bytes 50331652
Sparse Core Ops, SparseCore 0:
  166.6 55.9 all-reduce.3
  388.0 54.6 all-reduce.5
  608.1 54.6 all-reduce.7
where the time goes:
time: 724 us; the launch traced here: 713 us
  waiting for transfers between devices  296 us (41%)
  other arithmetic  210 us (29%)
  matrix products  124 us (17%)
  local copies, waits for them, and re-layouts  58.5 us (8%)
  between operations  14.2 us (2%)
  starting transfers between devices  10 us (1%)
    sub x6, other arithmetic, upwind_back(): return center - 0.5 * lam_col * (3.0 * center - 4.0 * nearer + farther)  187 us
    psum x3, waiting for transfers between devices, shards(): summed = lax.psum(raw_moments, 'vel')  165 us
    dot_general x3, matrix products, shards(): jnp.einsum('av,vxy->axy', table, weight * advected, precision=lax.Precisi...  70.1 us
    ppermute x3, waiting for transfers between devices, with_halo(): after = lax.ppermute(first, axis, down)  67.8 us
    ppermute x3, waiting for transfers between devices, with_halo(): before = lax.ppermute(last, axis, up)  63.2 us
    dot_general x3, matrix products, shards(): jnp.einsum('av,axy->vxy', table, coeffs, precision=lax.Precision.HIGHEST)  54.2 us
    unnamed x36, local copies, waits for them, and re-layouts  28.9 us
    unnamed x54, other arithmetic  18.7 us
  transfers between devices with their start and end apart: 9, of which 9 were waited for; matrix products, arithmetic and copies ran while one was open for 0% of the time, Pallas kernels for 0%

commit v1 on v0

--- a/solution.py
+++ b/solution.py
@@ -196,7 +196,9 @@
             "av,vxy->axy", table, weight * advected, precision=lax.Precision.HIGHEST
         )
         zero_cells = jnp.zeros_like(particle_concentration)
-        summed = lax.psum(raw_moments, "vel")
+        summed = raw_moments
+        for hop in (1, 2, 4):
+            summed = summed + lax.ppermute(summed, "vel", [(dev, dev ^ hop) for dev in range(8)])
         polys = hermite_polys(flow_rows, reciprocal_factor)
         coeffs = to_coeffs(to_modes(summed, polys, zero_cells), polys, zero_cells)
         returned = jnp.einsum("av,axy->vxy", table, coeffs, precision=lax.Precision.HIGHEST)

time: 724 us -> 606 us (0.84)
  waiting for transfers between devices: 296 us -> 205 us
  other arithmetic: 210 us -> 193 us
  starting transfers between devices: 10 us -> 23.7 us
  between operations: 14.2 us -> 0.92 us
    psum x3 -> x0, waiting for transfers between devices: 165 us -> none  [shards(): summed = lax.psum(raw_moments, 'vel')]
    ppermute x0 -> x9, waiting for transfers between devices: none -> 72.3 us  [shards(): lax.ppermute(summed, 'vel', [(dev, dev ^ hop) for dev in range(8)])]
    unnamed x54, other arithmetic: 18.7 us -> 1.73 us
    ppermute x0 -> x9, starting transfers between devices: none -> 14.8 us  [shards(): lax.ppermute(summed, 'vel', [(dev, dev ^ hop) for dev in range(8)])]
    unnamed x36 -> x26, local copies, waits for them, and re-layouts: 28.9 us -> 28.9 us
  transfers between devices with their start and end apart: 9 -> 15, of which waited for: 9 -> 15; matrix products, arithmetic and copies ran while one was open for 0% -> 0% of each run, Pallas kernels for 0% -> 0%
where the time goes in v1:
time: 606 us; the launch traced here: 601 us
  waiting for transfers between devices  205 us (34%)
  other arithmetic  193 us (32%)
  matrix products  123 us (20%)
  local copies, waits for them, and re-layouts  56.3 us (9%)
  starting transfers between devices  23.7 us (4%)
    sub x6, other arithmetic, upwind_back(): return center - 0.5 * lam_col * (3.0 * center - 4.0 * nearer + farther)  188 us
    ppermute x9, waiting for transfers between devices, shards(): lax.ppermute(summed, 'vel', [(dev, dev ^ hop) for dev in range(8)])  72.3 us
    dot_general x3, matrix products, shards(): jnp.einsum('av,vxy->axy', table, weight * advected, precision=lax.Precisi...  70.1 us
    ppermute x3, waiting for transfers between devices, with_halo(): after = lax.ppermute(first, axis, down)  68.2 us
    ppermute x3, waiting for transfers between devices, with_halo(): before = lax.ppermute(last, axis, up)  64.2 us
    dot_general x3, matrix products, shards(): jnp.einsum('av,axy->vxy', table, coeffs, precision=lax.Precision.HIGHEST)  52.6 us
    unnamed x26, local copies, waits for them, and re-layouts  28.9 us
    add x1, local copies, waits for them, and re-layouts, shards(): adjoint = (1.0 - relaxation_rate) * advected + relaxation_rate * returned  17.4 us
  transfers between devices with their start and end apart: 15, of which 15 were waited for; matrix products, arithmetic and copies ran while one was open for 0% of the time, Pallas kernels for 0%

profile of v1, /device:TPU:0, one launch (start us, length us, event | category | flops | bytes accessed | tf_op | source)
XLA Modules:
  0.0 601.5 jit_solution(15012369917515756597)
XLA Ops:
  0.0 0.7 broadcast_compare_fusion
  0.7 0.7 convert_multiply_fusion
  1.5 16.5 %copy.21 = f32[1024,32,128]{0,2,1:T(8,128)} copy(f32[1024,32,128]{2,1,0:T(8,128)} %param.4) | data formatting | bytes 33554432 | tf_op args[0]
  18.0 1.8 fusion.371
  19.8 0.6 slice_multiply_fusion.27
  20.4 34.8 %fusion.46 = f32[1024,32,128]{0,2,1:T(8,128)} fusion(f32[1024,32,128]{0,2,1:T(8,128)} %copy.21, f32[1024,32,2]{0,2,1:T(2,128)S(1)} %get-tuple-element.47, f32[1024,32,2]{0,2,1:T(2,128)S(1)} %get-tuple-element.46, f32[1024]{0:T(1024)S(1)} %bitcast.1794, pred[1024]{0:T(1024)(128)(4,1)S(1)} %get-tuple-element.6), kind=kLoop, calls=%fused_computation.70 | loop fusion | flops 50331648 | bytes 34083840 | tf_op jit(solution)/shard_map/sub | solution.py:151
  55.3 2.8 fusion.370
  58.0 3.9 collective-permute-start
  61.9 0.4 collective-permute-start.1
  62.4 0.6 slice_multiply_fusion.34
  63.0 1.5 stack.12
  64.6 0.6 multiply_bitcast_fusion
  65.2 20.6 %collective-permute-done = f32[1024,2,128]{0,2,1:T(8,128)S(1)} collective-permute-done((f32[1024,2,128]{0,2,1:T(8,128)}, f32[1024,2,128]{0,2,1:T(8,128)S(1)}, u32[]{:S(2)}, u32[]{:S(2)}) %collective-permute-start) | collective-permute-done | bytes 1048608 | tf_op jit(solution)/shard_map/ppermute | solution.py:43
  85.8 22.2 %collective-permute-done.1 = f32[1024,2,128]{0,2,1:T(8,128)S(1)} collective-permute-done((f32[1024,2,128]{0,2,1:T(8,128)S(1)}, f32[1024,2,128]{0,2,1:T(8,128)S(1)}, u32[]{:S(2)}, u32[]{:S(2)}) %collective-permute-start.1) | collective-permute-done | bytes 1048608 | tf_op jit(solution)/shard_map/ppermute | solution.py:42
  108.0 27.6 %fusion.38 = f32[1024,32,128]{0,2,1:T(8,128)S(1)} fusion(f32[1024,32,128]{0,2,1:T(8,128)} %fusion.46, f32[1024,2,128]{0,2,1:T(8,128)S(1)} %collective-permute-done.1, f32[1024,2,128]{0,2,1:T(8,128)S(1)} %collective-permute-done, f32[1024]{0:T(1024)S(1)} %bitcast.1791, pred[1024]{0:T(1024)(128)(4,1)S(1)} %get-tuple-element.5), kind=kLoop, calls=%fused_computation.62 | loop fusion | flops 50331648 | bytes 35656704 | tf_op jit(solution)/shard_map/sub | solution.py:151
  135.7 23.4 %fusion.86 = f32[20,32,128]{2,0,1:T(8,128)S(1)} fusion(f32[1024,32,128]{0,2,1:T(8,128)S(1)} %fusion.38, f32[32,128]{1,0:T(8,128)S(1)} %get-tuple-element.55, f32[1024]{0:T(1024)S(1)} %bitcast.1803, f32[32,128]{1,0:T(8,128)S(1)} %get-tuple-element.56, f32[1024]{0:T(1024)S(1)} %bitcast.1800, f32[32,128]{1,0:T(8,128)S(1)} %get-tuple-element.58, ...), kind=kOutput, calls=%fused_computation.125 | convolution fusion | flops 1065353216 | bytes 17281024 | tf_op jit(solution)/shard_map/av,vxy->axy/dot_general | solution.py:195
  159.0 0.1 copy.24
  159.1 0.1 collective-permute-start.2
  159.2 1.6 collective-permute-done.2
  160.8 0.1 copy_add_fusion.2
  160.9 1.6 collective-permute-start.3
  162.5 8.2 %collective-permute-done.3 = f32[20,32,128]{2,1,0:T(8,128)S(1)} collective-permute-done((f32[20,32,128]{2,1,0:T(8,128)S(1)}, f32[20,32,128]{2,1,0:T(8,128)S(1)}, u32[]{:S(2)}, u32[]{:S(2)}) %collective-permute-start.3) | collective-permute-done | bytes 327712 | tf_op jit(solution)/shard_map/ppermute | solution.py:201
  170.7 2.7 collective-permute-start.4
  173.4 14.2 %collective-permute-done.4 = f32[20,32,128]{2,1,0:T(8,128)S(1)} collective-permute-done((f32[20,32,128]{2,1,0:T(8,128)S(1)}, f32[20,32,128]{2,1,0:T(8,128)S(1)}, u32[]{:S(2)}, u32[]{:S(2)}) %collective-permute-start.4) | collective-permute-done | bytes 327712 | tf_op jit(solution)/shard_map/ppermute | solution.py:201
  187.7 0.2 constant_dynamic-update-slice_fusion.19
  188.4 17.5 %multiply_add_fusion.2 = f32[1024,32,128]{0,2,1:T(8,128)S(1)} fusion(f32[1024,32,128]{0,2,1:T(8,128)} %copy-done.2, f32[32,128]{1,0:T(8,128)S(1)} %get-tuple-element.64, f32[32,128]{1,0:T(8,128)S(1)} %get-tuple-element.63, f32[20,32,128]{2,1,0:T(8,128)S(1)} %constant_dynamic-update-slice_fusion, f32[20,1024]{1,0:T(8,128)S(1)} %stack.12), kind=kOutput, calls=%fused_computation.124 | convolution fusion | flops 1019215872 | bytes 33996800 | tf_op jit(solution)/shard_map/av,axy->vxy/dot_general | solution.py:204
  205.9 6.2 %copy-done.1 = f32[1024,32,128]{0,2,1:T(8,128)} copy-done((f32[1024,32,128]{0,2,1:T(8,128)}, f32[1024,32,128]{0,2,1:T(8,128)S(1)}, u32[]{:S(2)}) %copy-start.1) | copy-done | bytes 16777240
  212.1 0.2 fusion.369
  212.3 35.0 %fusion.30 = f32[1024,32,128]{0,2,1:T(8,128)} fusion(f32[1024,32,128]{0,2,1:T(8,128)} %copy-done.1, f32[1024,32,2]{0,2,1:T(2,128)S(1)} %get-tuple-element.43, f32[1024,32,2]{0,2,1:T(2,128)S(1)} %get-tuple-element.42, f32[1024]{0:T(1024)S(1)} %bitcast.1795, pred[1024]{0:T(1024)(128)(4,1)S(1)} %get-tuple-element.6), kind=kLoop, calls=%fused_computation.54 | loop fusion | flops 50331648 | bytes 34083840 | tf_op jit(solution)/shard_map/sub | solution.py:151
  247.3 1.7 fusion.368
  249.0 1.5 collective-permute-start.5
  250.5 0.6 collective-permute-start.6
  251.0 24.0 %collective-permute-done.5 = f32[1024,2,128]{0,2,1:T(8,128)S(1)} collective-permute-done((f32[1024,2,128]{0,2,1:T(8,128)S(1)}, f32[1024,2,128]{0,2,1:T(8,128)S(1)}, u32[]{:S(2)}, u32[]{:S(2)}) %collective-permute-start.5) | collective-permute-done | bytes 1048608 | tf_op jit(solution)/shard_map/ppermute | solution.py:43
  275.0 20.3 %collective-permute-done.6 = f32[1024,2,128]{0,2,1:T(8,128)S(1)} collective-permute-done((f32[1024,2,128]{0,2,1:T(8,128)S(1)}, f32[1024,2,128]{0,2,1:T(8,128)S(1)}, u32[]{:S(2)}, u32[]{:S(2)}) %collective-permute-start.6) | collective-permute-done | bytes 1048608 | tf_op jit(solution)/shard_map/ppermute | solution.py:42
  295.4 27.6 %fusion.22 = f32[1024,32,128]{0,2,1:T(8,128)S(1)} fusion(f32[1024,32,128]{0,2,1:T(8,128)} %fusion.30, f32[1024,2,128]{0,2,1:T(8,128)S(1)} %collective-permute-done.6, f32[1024,2,128]{0,2,1:T(8,128)S(1)} %collective-permute-done.5, f32[1024]{0:T(1024)S(1)} %bitcast.1792, pred[1024]{0:T(1024)(128)(4,1)S(1)} %get-tuple-element.5), kind=kLoop, calls=%fused_computation.46 | loop fusion | flops 50331648 | bytes 35656704 | tf_op jit(solution)/shard_map/sub | solution.py:151
  323.0 23.4 %fusion.70 = f32[20,32,128]{2,0,1:T(8,128)S(1)} fusion(f32[1024,32,128]{0,2,1:T(8,128)S(1)} %fusion.22, f32[32,128]{1,0:T(8,128)S(1)} %get-tuple-element.52, f32[32,128]{1,0:T(8,128)S(1)} %copy-done.5, f32[32,128]{1,0:T(8,128)S(1)} %copy-done.7, f32[32,128]{1,0:T(8,128)S(1)} %copy-done.6, f32[32,128]{1,0:T(8,128)S(1)} %get-tuple-element.49, ...), kind=kOutput, calls=%fused_computation.108 | convolution fusion | flops 1065353216 | bytes 17281024 | tf_op jit(solution)/shard_map/av,vxy->axy/dot_general | solution.py:195
  346.5 0.1 collective-permute-start.7
  346.6 1.6 collective-permute-done.7
  348.2 0.1 copy_add_fusion.1
  348.3 1.9 collective-permute-start.8
  350.1 8.0 %collective-permute-done.8 = f32[20,32,128]{2,1,0:T(8,128)S(1)} collective-permute-done((f32[20,32,128]{2,1,0:T(8,128)S(1)}, f32[20,32,128]{2,1,0:T(8,128)S(1)}, u32[]{:S(2)}, u32[]{:S(2)}) %collective-permute-start.8) | collective-permute-done | bytes 327712 | tf_op jit(solution)/shard_map/ppermute | solution.py:201
  358.2 3.4 collective-permute-start.9
  361.6 14.5 %collective-permute-done.9 = f32[20,32,128]{2,1,0:T(8,128)S(1)} collective-permute-done((f32[20,32,128]{2,1,0:T(8,128)S(1)}, f32[20,32,128]{2,1,0:T(8,128)S(1)}, u32[]{:S(2)}, u32[]{:S(2)}) %collective-permute-start.9) | collective-permute-done | bytes 327712 | tf_op jit(solution)/shard_map/ppermute | solution.py:201
  376.1 0.2 constant_dynamic-update-slice_fusion.39
  376.8 17.5 %multiply_add_fusion.1 = f32[1024,32,128]{0,2,1:T(8,128)S(1)} fusion(f32[1024,32,128]{0,2,1:T(8,128)} %copy-done.3, f32[32,128]{1,0:T(8,128)S(1)} %get-tuple-element.66, f32[32,128]{1,0:T(8,128)S(1)} %get-tuple-element.65, f32[20,32,128]{2,1,0:T(8,128)S(1)} %constant_dynamic-update-slice_fusion.20, f32[20,1024]{1,0:T(8,128)S(1)} %stack.12), kind=kOutput, calls=%fused_computation.107 | convolution fusion | flops 1019215872 | bytes 33996800 | tf_op jit(solution)/shard_map/av,axy->vxy/dot_general | solution.py:204
  394.4 6.2 %copy-done = f32[1024,32,128]{0,2,1:T(8,128)} copy-done((f32[1024,32,128]{0,2,1:T(8,128)}, f32[1024,32,128]{0,2,1:T(8,128)S(1)}, u32[]{:S(2)}) %copy-start) | copy-done | bytes 16777240
  400.5 0.2 fusion.367
  400.7 35.0 %fusion.14 = f32[1024,32,128]{0,2,1:T(8,128)} fusion(f32[1024,32,128]{0,2,1:T(8,128)} %copy-done, f32[1024,32,2]{0,2,1:T(2,128)S(1)} %get-tuple-element.39, f32[1024,32,2]{0,2,1:T(2,128)S(1)} %get-tuple-element.38, f32[1024]{0:T(1024)S(1)} %bitcast.1796, pred[1024]{0:T(1024)(128)(4,1)S(1)} %get-tuple-element.6), kind=kLoop, calls=%fused_computation.38 | loop fusion | flops 50331648 | bytes 34083840 | tf_op jit(solution)/shard_map/sub | solution.py:151
  435.8 1.7 fusion.366
  437.4 2.5 collective-permute-start.10
  439.9 23.6 %collective-permute-done.10 = f32[1024,2,128]{0,2,1:T(8,128)S(1)} collective-permute-done((f32[1024,2,128]{0,2,1:T(8,128)S(1)}, f32[1024,2,128]{0,2,1:T(8,128)S(1)}, u32[]{:S(2)}, u32[]{:S(2)}) %collective-permute-start.10) | collective-permute-done | bytes 1048608 | tf_op jit(solution)/shard_map/ppermute | solution.py:43
  463.5 21.6 %collective-permute-done.11 = f32[1024,2,128]{0,2,1:T(8,128)S(1)} collective-permute-done((f32[1024,2,128]{0,2,1:T(8,128)S(1)}, f32[1024,2,128]{0,2,1:T(8,128)S(1)}, u32[]{:S(2)}, u32[]{:S(2)}) %collective-permute-start.11) | collective-permute-done | bytes 1048608 | tf_op jit(solution)/shard_map/ppermute | solution.py:42
  485.1 27.6 %fusion.6 = f32[1024,32,128]{0,2,1:T(8,128)S(1)} fusion(f32[1024,32,128]{0,2,1:T(8,128)} %fusion.14, f32[1024,2,128]{0,2,1:T(8,128)S(1)} %collective-permute-done.11, f32[1024,2,128]{0,2,1:T(8,128)S(1)} %collective-permute-done.10, f32[1024]{0:T(1024)S(1)} %bitcast.1793, pred[1024]{0:T(1024)(128)(4,1)S(1)} %get-tuple-element.5), kind=kLoop, calls=%fused_computation.30 | loop fusion | flops 50331648 | bytes 35656704 | tf_op jit(solution)/shard_map/sub | solution.py:151
  512.7 23.4 %fusion.54 = f32[20,32,128]{2,0,1:T(8,128)S(1)} fusion(f32[1024,32,128]{0,2,1:T(8,128)S(1)} %fusion.6, f32[32,128]{1,0:T(8,128)S(1)} %get-tuple-element.61, f32[32,128]{1,0:T(8,128)S(1)} %get-tuple-element.62, f32[32,128]{1,0:T(8,128)S(1)} %get-tuple-element.60, f32[32,128]{1,0:T(8,128)S(1)} %get-tuple-element.51, f32[32,128]{1,0:T(8,128)S(1)} %get-tuple-element.48, ...), kind=kOutput, calls=%fused_computation.91 | convolution fusion | flops 1065353216 | bytes 17281024 | tf_op jit(solution)/shard_map/av,vxy->axy/dot_general | solution.py:195
  536.1 0.1 collective-permute-start.12
  536.2 1.6 collective-permute-done.12
  537.8 0.1 copy_add_fusion
  537.9 1.7 collective-permute-start.13
  539.6 8.1 %collective-permute-done.13 = f32[20,32,128]{2,1,0:T(8,128)S(1)} collective-permute-done((f32[20,32,128]{2,1,0:T(8,128)S(1)}, f32[20,32,128]{2,1,0:T(8,128)S(1)}, u32[]{:S(2)}, u32[]{:S(2)}) %collective-permute-start.13) | collective-permute-done | bytes 327712 | tf_op jit(solution)/shard_map/ppermute | solution.py:201
  547.8 3.3 collective-permute-start.14
  551.1 14.5 %collective-permute-done.14 = f32[20,32,128]{2,1,0:T(8,128)S(1)} collective-permute-done((f32[20,32,128]{2,1,0:T(8,128)S(1)}, f32[20,32,128]{2,1,0:T(8,128)S(1)}, u32[]{:S(2)}, u32[]{:S(2)}) %collective-permute-start.14) | collective-permute-done | bytes 327712 | tf_op jit(solution)/shard_map/ppermute | solution.py:201
  565.6 0.2 constant_dynamic-update-slice_fusion.59
  566.3 17.6 %multiply_add_fusion = f32[1024,32,128]{0,2,1:T(8,128)} fusion(f32[1024,32,128]{0,2,1:T(8,128)S(1)} %fusion.6, f32[32,128]{1,0:T(8,128)S(1)} %get-tuple-element.15, f32[32,128]{1,0:T(8,128)S(1)} %get-tuple-element.14, f32[20,32,128]{2,1,0:T(8,128)S(1)} %constant_dynamic-update-slice_fusion.40, f32[20,1024]{1,0:T(8,128)S(1)} %stack.12), kind=kOutput, calls=%fused_computation.90 | convolution fusion | flops 1019215872 | bytes 33996800 | tf_op jit(solution)/shard_map/av,axy->vxy/dot_general | solution.py:204
  583.9 17.4 %copy.35 = f32[1024,32,128]{2,1,0:T(8,128)} copy(f32[1024,32,128]{0,2,1:T(8,128)} %multiply_add_fusion) | data formatting | bytes 33554432 | tf_op jit(solution)/shard_map/add | solution.py:205
  (89 shorter events, 1.8 us)
Async XLA Ops:
  20.4 44.2 %copy-start.4 = (f32[3,5,32,128]{3,2,1,0:T(8,128)S(1)}, f32[3,5,32,128]{3,2,1,0:T(8,128)}, u32[]{:S(2)}) copy-start(f32[3,5,32,128]{3,2,1,0:T(8,128)} %param.7) | copy-start | bytes 737284
  58.0 27.8 %collective-permute-start = (f32[1024,2,128]{0,2,1:T(8,128)}, f32[1024,2,128]{0,2,1:T(8,128)S(1)}, u32[]{:S(2)}, u32[]{:S(2)}) collective-permute-start(f32[1024,2,128]{0,2,1:T(8,128)} %get-tuple-element.44), channel_id=1, source_target_pairs={{8,0},{16,8},{24,16},{0,24},{9,1},{17,9},{25,17},{1,25},{10,2},{18... | collective-permute-start | bytes 3145736 | tf_op jit(solution)/shard_map/ppermute | solution.py:43
  61.9 46.1 %collective-permute-start.1 = (f32[1024,2,128]{0,2,1:T(8,128)S(1)}, f32[1024,2,128]{0,2,1:T(8,128)S(1)}, u32[]{:S(2)}, u32[]{:S(2)}) collective-permute-start(f32[1024,2,128]{0,2,1:T(8,128)S(1)} %get-tuple-element.45), channel_id=1, source_target_pairs={{0,8},{8,16},{16,24},{24,0},{1,9},{9,17},{17,25},{25,1},{2,10},{10... | collective-permute-start | bytes 3145736 | tf_op jit(solution)/shard_map/ppermute | solution.py:42
  108.0 27.6 %copy-start.8 = (f32[1,1024]{1,0:T(1,128)S(1)}, f32[1,1024]{1,0:T(1,128)}, u32[]{:S(2)}) copy-start(f32[1,1024]{1,0:T(1,128)} %get-tuple-element.88) | copy-start | bytes 12292
  108.0 27.6 %copy-start.9 = (f32[1,1024]{1,0:T(1,128)S(1)}, f32[1,1024]{1,0:T(1,128)}, u32[]{:S(2)}) copy-start(f32[1,1024]{1,0:T(1,128)} %get-tuple-element.89) | copy-start | bytes 12292
  108.0 27.6 %copy-start.10 = (f32[1,1024]{1,0:T(1,128)S(1)}, f32[1,1024]{1,0:T(1,128)}, u32[]{:S(2)}) copy-start(f32[1,1024]{1,0:T(1,128)} %get-tuple-element.90) | copy-start | bytes 12292
  135.6 23.4 %copy-start.2 = (f32[1024,32,128]{0,2,1:T(8,128)}, f32[1024,32,128]{0,2,1:T(8,128)S(1)}, u32[]{:S(2)}) copy-start(f32[1024,32,128]{0,2,1:T(8,128)S(1)} %fusion.38) | copy-start | bytes 50331652
  159.1 1.7 collective-permute-start.2
  160.9 9.8 %collective-permute-start.3 = (f32[20,32,128]{2,1,0:T(8,128)S(1)}, f32[20,32,128]{2,1,0:T(8,128)S(1)}, u32[]{:S(2)}, u32[]{:S(2)}) collective-permute-start(f32[20,32,128]{2,1,0:T(8,128)S(1)} %copy_add_fusion.2), channel_id=1, source_target_pairs={{0,2},{1,3},{2,0},{3,1},{4,6},{5,7},{6,4},{7,5},{8,10},{9,11},{10,... | collective-permute-start | bytes 983048 | tf_op jit(solution)/shard_map/ppermute | solution.py:201
  170.7 16.9 %collective-permute-start.4 = (f32[20,32,128]{2,1,0:T(8,128)S(1)}, f32[20,32,128]{2,1,0:T(8,128)S(1)}, u32[]{:S(2)}, u32[]{:S(2)}) collective-permute-start(f32[20,32,128]{2,1,0:T(8,128)S(1)} %add.3972), channel_id=1, source_target_pairs={{0,4},{1,5},{2,6},{3,7},{4,0},{5,1},{6,2},{7,3},{8,12},{9,13},{10,... | collective-permute-start | bytes 983048 | tf_op jit(solution)/shard_map/ppermute | solution.py:201
  205.9 6.2 %copy-start.1 = (f32[1024,32,128]{0,2,1:T(8,128)}, f32[1024,32,128]{0,2,1:T(8,128)S(1)}, u32[]{:S(2)}) copy-start(f32[1024,32,128]{0,2,1:T(8,128)S(1)} %multiply_add_fusion.2) | copy-start | bytes 50331652
  249.0 26.1 %collective-permute-start.5 = (f32[1024,2,128]{0,2,1:T(8,128)S(1)}, f32[1024,2,128]{0,2,1:T(8,128)S(1)}, u32[]{:S(2)}, u32[]{:S(2)}) collective-permute-start(f32[1024,2,128]{0,2,1:T(8,128)S(1)} %get-tuple-element.40), channel_id=1, source_target_pairs={{8,0},{16,8},{24,16},{0,24},{9,1},{17,9},{25,17},{1,25},{10,2},{18... | collective-permute-start | bytes 3145736 | tf_op jit(solution)/shard_map/ppermute | solution.py:43
  250.4 72.5 %copy-start.5 = (f32[32,128]{1,0:T(8,128)S(1)}, f32[32,128]{1,0:T(8,128)}, u32[]{:S(2)}) copy-start(f32[32,128]{1,0:T(8,128)} %get-tuple-element.53) | copy-start | bytes 49156
  250.5 72.6 %copy-start.6 = (f32[32,128]{1,0:T(8,128)S(1)}, f32[32,128]{1,0:T(8,128)}, u32[]{:S(2)}) copy-start(f32[32,128]{1,0:T(8,128)} %get-tuple-element.54) | copy-start | bytes 49156
  250.5 72.6 %copy-start.7 = (f32[32,128]{1,0:T(8,128)S(1)}, f32[32,128]{1,0:T(8,128)}, u32[]{:S(2)}) copy-start(f32[32,128]{1,0:T(8,128)} %get-tuple-element.59) | copy-start | bytes 49156
  250.5 44.9 %collective-permute-start.6 = (f32[1024,2,128]{0,2,1:T(8,128)S(1)}, f32[1024,2,128]{0,2,1:T(8,128)S(1)}, u32[]{:S(2)}, u32[]{:S(2)}) collective-permute-start(f32[1024,2,128]{0,2,1:T(8,128)S(1)} %get-tuple-element.41), channel_id=1, source_target_pairs={{0,8},{8,16},{16,24},{24,0},{1,9},{9,17},{17,25},{25,1},{2,10},{10... | collective-permute-start | bytes 3145736 | tf_op jit(solution)/shard_map/ppermute | solution.py:42
  323.0 23.4 %copy-start.3 = (f32[1024,32,128]{0,2,1:T(8,128)}, f32[1024,32,128]{0,2,1:T(8,128)S(1)}, u32[]{:S(2)}) copy-start(f32[1024,32,128]{0,2,1:T(8,128)S(1)} %fusion.22) | copy-start | bytes 50331652
  346.5 1.7 collective-permute-start.7
  348.3 9.9 %collective-permute-start.8 = (f32[20,32,128]{2,1,0:T(8,128)S(1)}, f32[20,32,128]{2,1,0:T(8,128)S(1)}, u32[]{:S(2)}, u32[]{:S(2)}) collective-permute-start(f32[20,32,128]{2,1,0:T(8,128)S(1)} %copy_add_fusion.1), channel_id=1, source_target_pairs={{0,2},{1,3},{2,0},{3,1},{4,6},{5,7},{6,4},{7,5},{8,10},{9,11},{10,... | collective-permute-start | bytes 983048 | tf_op jit(solution)/shard_map/ppermute | solution.py:201
  358.2 17.9 %collective-permute-start.9 = (f32[20,32,128]{2,1,0:T(8,128)S(1)}, f32[20,32,128]{2,1,0:T(8,128)S(1)}, u32[]{:S(2)}, u32[]{:S(2)}) collective-permute-start(f32[20,32,128]{2,1,0:T(8,128)S(1)} %add.4112), channel_id=1, source_target_pairs={{0,4},{1,5},{2,6},{3,7},{4,0},{5,1},{6,2},{7,3},{8,12},{9,13},{10,... | collective-permute-start | bytes 983048 | tf_op jit(solution)/shard_map/ppermute | solution.py:201
  394.4 6.2 %copy-start = (f32[1024,32,128]{0,2,1:T(8,128)}, f32[1024,32,128]{0,2,1:T(8,128)S(1)}, u32[]{:S(2)}) copy-start(f32[1024,32,128]{0,2,1:T(8,128)S(1)} %multiply_add_fusion.1) | copy-start | bytes 50331652
  437.4 26.1 %collective-permute-start.10 = (f32[1024,2,128]{0,2,1:T(8,128)S(1)}, f32[1024,2,128]{0,2,1:T(8,128)S(1)}, u32[]{:S(2)}, u32[]{:S(2)}) collective-permute-start(f32[1024,2,128]{0,2,1:T(8,128)S(1)} %get-tuple-element.36), channel_id=1, source_target_pairs={{8,0},{16,8},{24,16},{0,24},{9,1},{17,9},{25,17},{1,25},{10,2},{18... | collective-permute-start | bytes 3145736 | tf_op jit(solution)/shard_map/ppermute | solution.py:43
  439.9 45.2 %collective-permute-start.11 = (f32[1024,2,128]{0,2,1:T(8,128)S(1)}, f32[1024,2,128]{0,2,1:T(8,128)S(1)}, u32[]{:S(2)}, u32[]{:S(2)}) collective-permute-start(f32[1024,2,128]{0,2,1:T(8,128)S(1)} %get-tuple-element.37), channel_id=1, source_target_pairs={{0,8},{8,16},{16,24},{24,0},{1,9},{9,17},{17,25},{25,1},{2,10},{10... | collective-permute-start | bytes 3145736 | tf_op jit(solution)/shard_map/ppermute | solution.py:42
  536.1 1.7 collective-permute-start.12
  537.9 9.8 %collective-permute-start.13 = (f32[20,32,128]{2,1,0:T(8,128)S(1)}, f32[20,32,128]{2,1,0:T(8,128)S(1)}, u32[]{:S(2)}, u32[]{:S(2)}) collective-permute-start(f32[20,32,128]{2,1,0:T(8,128)S(1)} %copy_add_fusion), channel_id=1, source_target_pairs={{0,2},{1,3},{2,0},{3,1},{4,6},{5,7},{6,4},{7,5},{8,10},{9,11},{10,... | collective-permute-start | bytes 983048 | tf_op jit(solution)/shard_map/ppermute | solution.py:201
  547.8 17.8 %collective-permute-start.14 = (f32[20,32,128]{2,1,0:T(8,128)S(1)}, f32[20,32,128]{2,1,0:T(8,128)S(1)}, u32[]{:S(2)}, u32[]{:S(2)}) collective-permute-start(f32[20,32,128]{2,1,0:T(8,128)S(1)} %add.4252), channel_id=1, source_target_pairs={{0,4},{1,5},{2,6},{3,7},{4,0},{5,1},{6,2},{7,3},{8,12},{9,13},{10,... | collective-permute-start | bytes 983048 | tf_op jit(solution)/shard_map/ppermute | solution.py:201
